TPU v7x, 128 devices: a whole 4x4x4 slice. The times are simulated.
128 devices in a mesh: gx: 8 (over z, core), gy: 16 (over x, y).
Axes of the slice: x: 4, y: 4, z: 4, core: 2. Of those that a mesh axis runs over, the one named last changes fastest.
Arguments:
- tokens: bfloat16 [4096, 4096], P(('gx', 'gy')), may hold values from -3 to 3
- attn_gain: bfloat16 [4096], replicated, may hold values from 0.099609375 to 1.8984375
- mlp_gain: bfloat16 [4096], replicated, may hold values from 0.099609375 to 1.8984375
- w_query: bfloat16 [4096, 4096], P('gx', 'gy'), may hold values from -1 to 1
- w_key: bfloat16 [4096, 1024], P('gx', 'gy'), may hold values from -1 to 1
- value_projection: bfloat16 [4096, 1024], P('gx', 'gy'), may hold values from -0.09375 to 0.09375
- w_out: bfloat16 [4096, 4096], P('gy', 'gx'), may hold values from -0.09375 to 0.09375
- w_gate: bfloat16 [4096, 14336], P('gx', 'gy'), may hold values from -0.09375 to 0.09375
- w_up: bfloat16 [4096, 14336], P('gx', 'gy'), may hold values from -0.09375 to 0.09375
- w_down: bfloat16 [14336, 4096], P('gy', 'gx'), may hold values from -0.046875 to 0.046875
- lengths: int32 [6], replicated, may hold values from 1 to 3072, 4096 in all
- page_table: int32 [128, 2], replicated, may hold values from 0 to 15, as said below
Outputs:
- layer_out: bfloat16 [4096, 4096], P(('gx', 'gy'))
- paged_key_value_cache: bfloat16 [128, 2, 32, 1024], P('gx', None, None, 'gy')
Inputs may be any that keep to these rules, and one draw needn't show every extreme that they name: `page_table`: page p belongs to token group p // 16, the tokens of one index of gx. Its owner is an index of gx and its slot is below 16; every pair of owner and slot is taken by exactly one page. Of one token group's pages, 8 owners receive exactly 2 each and the other owners none.
All inputs are finite; a program needn't handle non-finite values.
Results may differ from a plain program's by a relative error of at most 0.025.
The roundings to bfloat16 on the way count: a program that leaves them out, or rounds other values in their place, can miss the bound.
Values may be sent and summed in bfloat16 or wider, within the bound.
A program may use at most 128 MiB of HBM per device.

v0:
```python
import jax
import jax.numpy as jnp
from jax import lax
from jax.sharding import PartitionSpec as P

HEAD_WIDTH = 128
WIN = 4096
PAGE_TOKENS = 32
rope_base = 10000.0
norm_eps = 1e-05
masked_score = -1e30


def partner(value, axis, distance):
    mask = 2**distance
    pairs = [(source, source ^ mask) for source in range(lax.axis_size(axis))]
    return lax.ppermute(value, axis, pairs)


def rms_scale(values, gain):
    floats = values.astype(jnp.float32)
    mean_square = jnp.mean(floats * floats, axis=-1, keepdims=True)
    return floats * lax.rsqrt(mean_square + norm_eps) * gain.astype(jnp.float32)


def segment_info(lengths, token_index):
    ends = jnp.cumsum(lengths, dtype=jnp.int32)
    starts = ends - lengths
    inside = (token_index[:, None] >= starts[None, :]).astype(jnp.int32)
    segment = jnp.sum(inside, axis=1, dtype=jnp.int32) - 1
    chosen = (segment[:, None] == jnp.arange(lengths.shape[0], dtype=jnp.int32)[None, :]).astype(
        jnp.int32
    )
    token_positions = token_index - jnp.sum(chosen * starts[None, :], axis=1, dtype=jnp.int32)
    return (segment, token_positions)


def apply_rotary(values, token_positions):
    half = values.shape[-1] // 2
    freq = rope_base ** (-jnp.arange(half, dtype=jnp.float32) * 2.0 / values.shape[-1])
    angle = token_positions.astype(jnp.float32)[:, None] * freq[None, :]
    cosine = jnp.cos(angle)[:, None, :]
    sine = jnp.sin(angle)[:, None, :]
    first = values[..., :half]
    second = values[..., half:]
    return jnp.concatenate(
        [first * cosine - second * sine, second * cosine + first * sine], axis=-1
    )


def join_halves(mine, other, lower):
    return jnp.where(
        lower, jnp.concatenate([mine, other], axis=1), jnp.concatenate([other, mine], axis=1)
    )


def row_products(source, pieces):
    return tuple((jnp.dot(source, piece, preferred_element_type=jnp.float32) for piece in pieces))


def per_device(
    tokens,
    attn_gain,
    mlp_gain,
    w_query,
    w_key,
    value_projection,
    w_out,
    w_gate,
    w_up,
    w_down,
    lengths,
    page_table,
):
    group_count = lax.axis_size("gx")
    local_rows = tokens.shape[0]
    group = local_rows * lax.axis_size("gy")
    group_index = lax.axis_index("gx")
    head_index = lax.axis_index("gy")
    group_start = group_index * group
    lower = head_index % 2 == 0
    query_cols = w_query.shape[1]
    query_heads = query_cols // HEAD_WIDTH
    key_cols = w_key.shape[1]
    key_heads = max(1, key_cols // HEAD_WIDTH)
    per_key = query_heads // key_heads
    normed = lax.all_gather(
        rms_scale(tokens, attn_gain).astype(jnp.bfloat16), "gy", axis=0, tiled=True
    )
    query = row_products(normed, (lax.all_gather(w_query, "gx", axis=0, tiled=True),))[0]
    key_weight, value_weight = (w_key, value_projection)
    unrotated_key, value_raw = row_products(
        normed,
        (
            lax.all_gather(key_weight, "gx", axis=0, tiled=True),
            lax.all_gather(value_weight, "gx", axis=0, tiled=True),
        ),
    )
    other_key, other_value = (
        partner(unrotated_key.astype(jnp.bfloat16), "gy", 0).astype(unrotated_key.dtype),
        partner(value_raw.astype(jnp.bfloat16), "gy", 0).astype(value_raw.dtype),
    )
    unrotated_key = join_halves(unrotated_key, other_key, lower)
    value_raw = join_halves(value_raw, other_value, lower)
    token_index = group_start + jnp.arange(group, dtype=jnp.int32)
    segment, token_positions = segment_info(lengths, token_index)
    query_rot = (
        apply_rotary(query.reshape(group, query_heads, HEAD_WIDTH), token_positions)
        .astype(jnp.bfloat16)
        .reshape(group, key_heads, per_key, HEAD_WIDTH)
    )
    rotated_key = (
        apply_rotary(unrotated_key.reshape(group, key_heads, HEAD_WIDTH), token_positions)
        .astype(jnp.bfloat16)
        .reshape(group, key_heads * HEAD_WIDTH)
    )
    value_vectors = value_raw.astype(jnp.bfloat16)
    scale = HEAD_WIDTH ** (-0.5)
    start_state = (
        jnp.full((key_heads, per_key, group), masked_score, jnp.float32),
        jnp.zeros((key_heads, per_key, group), jnp.float32),
        jnp.zeros((key_heads, per_key, group, HEAD_WIDTH), jnp.float32),
    )
    keys = lax.all_gather(rotated_key, "gx", axis=0, tiled=True)
    values = lax.all_gather(value_vectors, "gx", axis=0, tiled=True)
    count = keys.shape[0]
    key_index = jnp.arange(count, dtype=jnp.int32)
    key_segment, unused = segment_info(lengths, key_index)
    distance = token_index[:, None] - key_index[None, :]
    allowed = (segment[:, None] == key_segment[None, :]) & (distance >= 0) & (distance < WIN)

    def update(state):
        running, total, weighted = state
        scores = (
            jnp.einsum(
                "qhgd,khd->hgqk",
                query_rot,
                keys.reshape(count, key_heads, HEAD_WIDTH),
                preferred_element_type=jnp.float32,
            )
            * scale
        )
        masked = jnp.where(allowed[None, None], scores, masked_score)
        newest = jnp.maximum(running, jnp.max(masked, axis=-1))
        weights = jnp.where(allowed[None, None], jnp.exp(masked - newest[..., None]), 0.0)
        mixed = jnp.einsum(
            "hgqk,khd->hgqd",
            weights.astype(jnp.bfloat16),
            values.reshape(count, key_heads, HEAD_WIDTH),
            preferred_element_type=jnp.float32,
        )
        return (newest, jnp.sum(weights, axis=-1), mixed)

    state = lax.cond(jnp.any(allowed), update, lambda state: state, start_state)
    attended = (state[2] / state[1][..., None]).astype(jnp.bfloat16)
    attended = attended.transpose(2, 0, 1, 3).reshape(group, query_cols)
    partial_value = jnp.dot(
        attended,
        lax.all_gather(w_out, "gx", axis=1, tiled=True),
        preferred_element_type=jnp.float32,
    )
    share = lax.psum_scatter(
        partial_value.astype(jnp.bfloat16), "gy", scatter_dimension=0, tiled=True
    ).astype(jnp.float32)
    residual = (tokens.astype(jnp.float32) + share).astype(jnp.bfloat16)
    mlp_input = lax.all_gather(
        rms_scale(residual, mlp_gain).astype(jnp.bfloat16), "gy", axis=0, tiled=True
    )
    gate, up_values = row_products(
        mlp_input,
        (
            lax.all_gather(w_gate, "gx", axis=0, tiled=True),
            lax.all_gather(w_up, "gx", axis=0, tiled=True),
        ),
    )
    hidden = (jax.nn.silu(gate) * up_values).astype(jnp.bfloat16)
    down_full = lax.all_gather(w_down, "gx", axis=1, tiled=True)
    mlp_share = lax.psum_scatter(
        jnp.dot(hidden, down_full, preferred_element_type=jnp.float32).astype(jnp.bfloat16),
        "gy",
        scatter_dimension=0,
        tiled=True,
    ).astype(jnp.float32)
    layer_out = (residual.astype(jnp.float32) + mlp_share).astype(jnp.bfloat16)
    own_start = jnp.where(lower, 0, key_cols).astype(jnp.int32)
    local_key = lax.dynamic_slice_in_dim(rotated_key, own_start, key_cols, 1)
    own_value = lax.dynamic_slice_in_dim(value_vectors, own_start, key_cols, 1)
    slots_group = group // PAGE_TOKENS
    capacity = max(2, slots_group // group_count)
    pages_local = (
        jnp.stack([local_key, own_value], axis=0)
        .reshape(2, slots_group, PAGE_TOKENS, key_cols)
        .transpose(1, 0, 2, 3)
        .reshape(slots_group, 2 * PAGE_TOKENS * key_cols)
    )
    owner = page_table[:, 0]
    slot = page_table[:, 1]
    page_index = jnp.arange(owner.shape[0], dtype=jnp.int32)
    page_group = page_index // slots_group
    before = (
        (page_group[:, None] == page_group[None, :])
        & (owner[:, None] == owner[None, :])
        & (page_index[None, :] < page_index[:, None])
    )
    rank = jnp.sum(before.astype(jnp.int32), axis=1, dtype=jnp.int32)
    my_owner = lax.dynamic_slice_in_dim(owner, group_index * slots_group, slots_group, 0)
    my_rank = lax.dynamic_slice_in_dim(rank, group_index * slots_group, slots_group, 0)
    target = jnp.arange(group_count * capacity, dtype=jnp.int32)
    select = (
        (my_owner[None, :] == target[:, None] // capacity)
        & (my_rank[None, :] == target[:, None] % capacity)
    ).astype(jnp.bfloat16)
    outgoing = (
        jnp.dot(select, pages_local, preferred_element_type=jnp.float32)
        .astype(jnp.bfloat16)
        .reshape(group_count, capacity, 2, PAGE_TOKENS, key_cols)
    )
    incoming = lax.all_to_all(outgoing, "gx", split_axis=0, concat_axis=0, tiled=True)
    column = page_group * capacity + rank
    pick = (
        (owner[None, :] == group_index)
        & (slot[None, :] == jnp.arange(slots_group, dtype=jnp.int32)[:, None])
    ).astype(jnp.float32)
    place = (column[:, None] == target[None, :]).astype(jnp.float32)
    routing = jnp.dot(pick, place, preferred_element_type=jnp.float32).astype(jnp.bfloat16)
    paged_key_value_cache = (
        jnp.dot(
            routing,
            incoming.reshape(group_count * capacity, 2 * PAGE_TOKENS * key_cols),
            preferred_element_type=jnp.float32,
        )
        .astype(jnp.bfloat16)
        .reshape(slots_group, 2, PAGE_TOKENS, key_cols)
    )
    return (layer_out, paged_key_value_cache)


def solution(mesh):
    placed = (
        P(("gx", "gy"), None),
        P(),
        P(),
        P("gx", "gy"),
        P("gx", "gy"),
        P("gx", "gy"),
        P("gy", "gx"),
        P("gx", "gy"),
        P("gx", "gy"),
        P("gy", "gx"),
        P(),
        P(),
    )
    return jax.shard_map(
        per_device,
        mesh=mesh,
        in_specs=placed,
        out_specs=(P(("gx", "gy"), None), P("gx", None, None, "gy")),
        check_vma=False,
    )
```

profile of v0, /device:TPU:0, one launch (start us, length us, event | category | flops | bytes accessed | tf_op | source)
XLA Modules:
  0.0 550.2 jit_solution(15981981439846609788)
XLA Ops:
  9.1 1.8 fusion.23
  13.4 14.6 %all_gather.35 = bf16[4096,64]{0,1:T(8,128)(2,1)S(1)} all-gather(bf16[512,64]{0,1:T(8,128)(2,1)} %param.18), channel_id=1, replica_groups=mesh['gx'=8,'gy'=16] {'gx'}, dimensions={0}, use_global_device_ids=true | all-gather | bytes 589824 | tf_op jit(solution)/shard_map/all_gather | solution.py:95
  28.0 36.9 %all-gather.10.cloned.1.call-done = bf16[512,4096]{1,0:T(8,128)(2,1)} async-done(((bf16[32,4096]{1,0:T(8,128)(2,1)}), bf16[512,4096]{1,0:T(8,128)(2,1)}) %all-gather.10.cloned.1.call-update) | async-done | bytes 4194320 | tf_op jit(solution)/shard_map/all_gather | solution.py:87
  64.9 3.6 fusion.62
  70.0 2.8 collective-permute-done
  74.2 14.2 %all_gather.37 = bf16[4096,64]{0,1:T(8,128)(2,1)S(1)} all-gather(bf16[512,64]{0,1:T(8,128)(2,1)S(1)} %copy-done.3), channel_id=1, replica_groups=mesh['gx'=8,'gy'=16] {'gx'}, dimensions={0}, use_global_device_ids=true | all-gather | bytes 589824 | tf_op jit(solution)/shard_map/all_gather | solution.py:96
  88.3 3.7 fusion.64
  92.0 1.8 collective-permute-start.1
  93.8 2.6 collective-permute-done.1
  97.9 3.6 fusion.20
  102.1 1.8 multiply_cosine_fusion
  103.9 4.2 fusion.63
  109.9 7.8 %all-gather.14.cloned.1.call-done = bf16[4096,128]{0,1:T(8,128)(2,1)} async-done(((bf16[512,128]{0,1:T(8,128)(2,1)}), bf16[4096,128]{0,1:T(8,128)(2,1)}) %all-gather.14.cloned.1.call-update) | async-done | bytes 1048592 | tf_op jit(solution)/shard_map/all_gather | solution.py:124
  117.7 25.0 %all-gather.16.cloned.1.call-done = bf16[4096,128]{0,1:T(8,128)(2,1)} async-done(((bf16[512,128]{0,1:T(8,128)(2,1)}), bf16[4096,128]{0,1:T(8,128)(2,1)}) %all-gather.16.cloned.1.call-update) | async-done | bytes 1048592 | tf_op jit(solution)/shard_map/all_gather | solution.py:125
  142.8 14.2 %conditional.1 = (f32[1,2,512]{2,1,0:T(2,128)S(1)}, f32[1,2,512,128]{2,3,1,0:T(8,128)S(1)}) conditional(s32[]{:T(128)} %convert_element_type.114, () %tuple.16, (pred[512,4096]{0,1:T(8,128)(4,1)S(1)}, bf16[512,1,2,128]{3,0,2,1:T(8,128)(2,1)S(1)}, bf16[4096,128]{0,1:T(8,128)(2,1)}, bf16[4096,128]{0,1:T(8,128)(2,1)}) %tuple.17), branch_computations={%region_6.7_spmd, %region_7.10_spmd} | conditional | flops 2202008576 | bytes 63725612 | solution.py:154
  142.8 5.1 fusion
  147.9 4.6 fusion.7
  152.5 4.4 fusion.2
  157.0 12.6 %all-gather.18.cloned.1.call-done = bf16[256,4096]{1,0:T(8,128)(2,1)} async-done(((bf16[256,512]{1,0:T(8,128)(2,1)}), bf16[256,4096]{1,0:T(8,128)(2,1)}) %all-gather.18.cloned.1.call-update) | async-done | bytes 2097168 | tf_op jit(solution)/shard_map/all_gather | solution.py:159
  169.6 4.9 convolution_convert_fusion.1
  175.4 77.2 %reduce-scatter.3.cloned.1.call-done = bf16[32,4096]{1,0:T(8,128)(2,1)} async-done(((bf16[512,4096]{1,0:T(8,128)(2,1)}), bf16[32,4096]{1,0:T(8,128)(2,1)}) %reduce-scatter.3.cloned.1.call-update) | async-done | bytes 262160 | tf_op jit(solution)/shard_map/reduce_scatter | solution.py:162
  253.7 1.8 fusion.27
  257.1 42.2 %all-gather.22.cloned.1.call-done = bf16[4096,896]{1,0:T(8,128)(2,1)} async-done(((bf16[512,896]{1,0:T(8,128)(2,1)}), bf16[4096,896]{1,0:T(8,128)(2,1)}) %all-gather.22.cloned.1.call-update) | async-done | bytes 7340048 | tf_op jit(solution)/shard_map/all_gather | solution.py:172
  299.4 54.3 %all-gather.20.cloned.1.call-done = bf16[512,4096]{1,0:T(8,128)(2,1)} async-done(((bf16[32,4096]{1,0:T(8,128)(2,1)}), bf16[512,4096]{1,0:T(8,128)(2,1)}) %all-gather.20.cloned.1.call-update) | async-done | bytes 4194320 | tf_op jit(solution)/shard_map/all_gather | solution.py:166
  353.7 9.8 %fusion.65 = f32[512,896]{1,0:T(8,128)S(1)} fusion(bf16[512,4096]{1,0:T(8,128)(2,1)} %all-gather.20.cloned.1.call-done, bf16[4096,896]{1,0:T(8,128)(2,1)} %all-gather.22.cloned.1.call-done), kind=kOutput, calls=%fused_computation.120 | convolution fusion | flops 3758096384 | bytes 13369344 | tf_op jit(solution)/shard_map/dot_general | solution.py:58
  363.5 37.2 %all-gather.24.cloned.1.call-done = bf16[4096,896]{1,0:T(8,128)(2,1)} async-done(((bf16[512,896]{1,0:T(8,128)(2,1)}), bf16[4096,896]{1,0:T(8,128)(2,1)}) %all-gather.24.cloned.1.call-update) | async-done | bytes 7340048 | tf_op jit(solution)/shard_map/all_gather | solution.py:173
  400.8 47.2 %all-gather.26.cloned.1.call-done = bf16[896,4096]{1,0:T(8,128)(2,1)} async-done(((bf16[896,512]{1,0:T(8,128)(2,1)}), bf16[896,4096]{1,0:T(8,128)(2,1)}) %all-gather.26.cloned.1.call-update) | async-done | bytes 7340048 | tf_op jit(solution)/shard_map/all_gather | solution.py:177
  448.0 16.3 %convolution_convert_fusion = bf16[512,4096]{1,0:T(8,128)(2,1)} fusion(bf16[896,4096]{1,0:T(8,128)(2,1)} %all-gather.26.cloned.1.call-done, f32[512,896]{1,0:T(8,128)S(1)} %fusion.65, bf16[512,4096]{1,0:T(8,128)(2,1)} %all-gather.20.cloned.1.call-done, bf16[4096,896]{1,0:T(8,128)(2,1)} %all-gather.24.cloned.1.call-done), kind=kOutput, calls=%fused_computation.22 | convolution fusion | flops 7521042432 | bytes 24903680 | tf_op jit(solution)/shard_map/dot_general | solution.py:179
  467.4 3.4 all-to-all-start
  470.7 6.0 %all-to-all-done = bf16[8,2,4096]{2,1,0:T(2,128)(2,1)S(1)} async-done(((bf16[8,2,4096]{2,1,0:T(2,128)(2,1)}), bf16[8,2,4096]{2,1,0:T(2,128)(2,1)S(1)}, u32[]{:S(2)}, u32[]{:S(2)}) %all-to-all-start) | async-done | bytes 131104 | tf_op jit(solution)/shard_map/all_to_all | solution.py:218
  478.6 63.3 %reduce-scatter.5.cloned.1.call-done = bf16[32,4096]{1,0:T(8,128)(2,1)} async-done(((bf16[512,4096]{1,0:T(8,128)(2,1)}), bf16[32,4096]{1,0:T(8,128)(2,1)}) %reduce-scatter.5.cloned.1.call-update) | async-done | bytes 262160 | tf_op jit(solution)/shard_map/reduce_scatter | solution.py:178
  541.9 1.7 fusion.28
  (88 shorter events, 18.8 us)
Async XLA Ops:
  7.2 57.7 %all-gather.10.cloned.1.call-start = ((), (), s32[]{:S(2)}) async-start(), calls=%async_computation.3 | async-start | bytes 4456448 | tf_op jit(solution)/shard_map/all_gather | solution.py:87
  7.9 66.3 %copy-start.3 = (bf16[512,64]{0,1:T(8,128)(2,1)S(1)}, bf16[512,64]{0,1:T(8,128)(2,1)}, u32[]{:S(2)}) copy-start(bf16[512,64]{0,1:T(8,128)(2,1)} %param.19) | copy-start | bytes 196612
  10.9 93.0 %all-gather.12.cloned.1.call-start = ((), (), s32[]{:S(2)}) async-start(), calls=%async_computation.4 | async-start | bytes 2359296 | tf_op jit(solution)/shard_map/all_gather | solution.py:90
  11.6 106.1 %all-gather.14.cloned.1.call-start = ((), (), s32[]{:S(2)}) async-start(), calls=%async_computation.5 | async-start | bytes 1179648 | tf_op jit(solution)/shard_map/all_gather | solution.py:124
  68.5 4.3 collective-permute-start
  74.1 68.7 %all-gather.16.cloned.1.call-start = ((), (), s32[]{:S(2)}) async-start(), calls=%async_computation.6 | async-start | bytes 1179648 | tf_op jit(solution)/shard_map/all_gather | solution.py:125
  92.0 4.4 collective-permute-start.1
  97.1 72.5 %all-gather.18.cloned.1.call-start = ((), (), s32[]{:S(2)}) async-start(), calls=%async_computation.7 | async-start | bytes 2359296 | tf_op jit(solution)/shard_map/all_gather | solution.py:159
  97.7 154.9 %reduce-scatter.3.cloned.1.call-start = ((), (), s32[]{:S(2)}) async-start(), calls=%async_computation.8 | async-start | bytes 4456448 | tf_op jit(solution)/shard_map/reduce_scatter | solution.py:162
  142.8 5.2 copy-start.6
  174.6 0.8 copy-start.4
  174.6 78.0 %copy-start = (bf16[32,4096]{1,0:T(8,128)(2,1)S(1)}, bf16[32,4096]{1,0:T(8,128)(2,1)}, u32[]{:S(2)}) copy-start(bf16[32,4096]{1,0:T(8,128)(2,1)} %param.14) | copy-start | bytes 786436
  174.6 124.8 %all-gather.22.cloned.1.call-start = ((), (), s32[]{:S(2)}) async-start(), calls=%async_computation.10 | async-start | bytes 8257536 | tf_op jit(solution)/shard_map/all_gather | solution.py:172
  175.3 178.4 %all-gather.20.cloned.1.call-start = ((), (), s32[]{:S(2)}) async-start(), calls=%async_computation.9 | async-start | bytes 4456448 | tf_op jit(solution)/shard_map/all_gather | solution.py:166
  255.5 145.2 %all-gather.24.cloned.1.call-start = ((), (), s32[]{:S(2)}) async-start(), calls=%async_computation.11 | async-start | bytes 8257536 | tf_op jit(solution)/shard_map/all_gather | solution.py:173
  256.3 191.7 %all-gather.26.cloned.1.call-start = ((), (), s32[]{:S(2)}) async-start(), calls=%async_computation.12 | async-start | bytes 8257536 | tf_op jit(solution)/shard_map/all_gather | solution.py:177
  256.9 285.0 %reduce-scatter.5.cloned.1.call-start = ((), (), s32[]{:S(2)}) async-start(), calls=%async_computation.13 | async-start | bytes 4456448 | tf_op jit(solution)/shard_map/reduce_scatter | solution.py:178
  464.2 0.7 copy-start.5
  464.2 1.2 copy-start.2
  464.2 77.7 %copy-start.1 = (bf16[32,4096]{1,0:T(8,128)(2,1)S(1)}, bf16[32,4096]{1,0:T(8,128)(2,1)}, u32[]{:S(2)}) copy-start(bf16[32,4096]{1,0:T(8,128)(2,1)} %reduce-scatter.3.cloned.1.call-done) | copy-start | bytes 786436
  467.4 9.4 %all-to-all-start = ((bf16[8,2,4096]{2,1,0:T(2,128)(2,1)}), bf16[8,2,4096]{2,1,0:T(2,128)(2,1)S(1)}, u32[]{:S(2)}, u32[]{:S(2)}) async-start(bf16[8,2,4096]{2,1,0:T(2,128)(2,1)} %reshape.453), calls=%async_computation.2 | async-start | bytes 262144 | tf_op jit(solution)/shard_map/all_to_all | solution.py:218
Sparse Core Ops, SparseCore 0:
  11.0 53.8 all-gather.9
  66.6 25.7 all-gather.11
  94.1 23.5 all-gather.13
  119.3 23.4 all-gather.15
  144.3 25.2 all-gather.17
  174.7 77.8 reduce-scatter.2
  254.4 44.9 all-gather.21
  302.3 51.3 all-gather.19
  355.5 45.2 all-gather.23
  402.4 45.4 all-gather.25
  464.4 77.4 reduce-scatter.4
where the time goes:
time: 551 us; the launch traced here: 550 us
  waiting for transfers between devices  419 us (76%)
  matrix products  52.7 us (10%)
  blocking collectives  28.8 us (5%)
  other arithmetic  23.6 us (4%)
  between operations  14.8 us (3%)
  starting transfers between devices  7.29 us (1%)
    reduce_scatter x1, waiting for transfers between devices, per_device(): lax.psum_scatter(partial_value.astype(jnp.bfloat16), 'gy', scatter_dimens...  77.2 us
    reduce_scatter x1, waiting for transfers between devices, per_device(): lax.psum_scatter(jnp.dot(hidden, down_full, preferred_element_type=jnp.fl...  63.3 us
    all_gather x1, waiting for transfers between devices, per_device(): lax.all_gather(rms_scale(residual, mlp_gain).astype(jnp.bfloat16), 'gy',...  54.3 us
    all_gather x1, waiting for transfers between devices, per_device(): down_full = lax.all_gather(w_down, 'gx', axis=1, tiled=True)  47.2 us
    all_gather x1, waiting for transfers between devices, per_device(): lax.all_gather(w_gate, 'gx', axis=0, tiled=True)  42.2 us
    all_gather x1, waiting for transfers between devices, per_device(): lax.all_gather(w_up, 'gx', axis=0, tiled=True)  37.2 us
    all_gather x1, waiting for transfers between devices, per_device(): lax.all_gather(rms_scale(tokens, attn_gain).astype(jnp.bfloat16), 'gy', a...  36.9 us
    all_gather x1, waiting for transfers between devices, per_device(): values = lax.all_gather(value_vectors, 'gx', axis=0, tiled=True)  25 us
  transfers between devices with their start and end apart: 14, of which 13 were waited for; matrix products, arithmetic and copies ran while one was open for 10% of the time, Pallas kernels for 0%

commit v1 on v0

--- a/solution.py
+++ b/solution.py
@@ -169,7 +169,9 @@
     gate, up_values = row_products(
         mlp_input,
         (
-            lax.all_gather(w_gate, "gx", axis=0, tiled=True),
+            jnp.concatenate(
+                lax.all_to_all(jnp.stack([w_gate] * lax.axis_size("gx")), "gx", 0, 0), axis=0
+            ),
             lax.all_gather(w_up, "gx", axis=0, tiled=True),
         ),
     )

time: 551 us -> 526 us (0.955)
  waiting for transfers between devices: 419 us -> 280 us
  blocking collectives: 28.8 us -> 142 us
    all_to_all x0 -> x1, blocking collectives: none -> 113 us  [per_device(): lax.all_to_all(jnp.stack([w_gate] * lax.axis_size('gx')), 'gx', 0, 0)]
    all_gather x1, waiting for transfers between devices: 54.3 us -> 0.01 us  [per_device(): lax.all_gather(rms_scale(residual, mlp_gain).astype(jnp.bfloat16), 'gy',...]
    all_gather x1 -> x0, waiting for transfers between devices: 42.2 us -> none  [per_device(): lax.all_gather(w_gate, 'gx', axis=0, tiled=True)]
    all_gather x1, waiting for transfers between devices: 37.2 us -> 0.02 us  [per_device(): lax.all_gather(w_up, 'gx', axis=0, tiled=True)]
    all_gather x1, waiting for transfers between devices: 47.2 us -> 41.6 us  [per_device(): down_full = lax.all_gather(w_down, 'gx', axis=1, tiled=True)]
  transfers between devices with their start and end apart: 14 -> 13, of which waited for: 13 -> 10; matrix products, arithmetic and copies ran while one was open for 10% -> 10% of each run, Pallas kernels for 0% -> 0%
where the time goes in v1:
time: 526 us; the launch traced here: 525 us
  waiting for transfers between devices  280 us (53%)
  blocking collectives  142 us (27%)
  matrix products  52.7 us (10%)
  other arithmetic  23.6 us (4%)
  between operations  15.1 us (3%)
  starting transfers between devices  7.07 us (1%)
  local copies, waits for them, and re-layouts  5.31 us (1%)
    all_to_all x1, blocking collectives, per_device(): lax.all_to_all(jnp.stack([w_gate] * lax.axis_size('gx')), 'gx', 0, 0)  113 us
    reduce_scatter x1, waiting for transfers between devices, per_device(): lax.psum_scatter(partial_value.astype(jnp.bfloat16), 'gy', scatter_dimens...  77.9 us
    reduce_scatter x1, waiting for transfers between devices, per_device(): lax.psum_scatter(jnp.dot(hidden, down_full, preferred_element_type=jnp.fl...  63.3 us
    all_gather x1, waiting for transfers between devices, per_device(): down_full = lax.all_gather(w_down, 'gx', axis=1, tiled=True)  41.6 us
    all_gather x1, waiting for transfers between devices, per_device(): lax.all_gather(rms_scale(tokens, attn_gain).astype(jnp.bfloat16), 'gy', a...  36.9 us
    all_gather x1, waiting for transfers between devices, per_device(): values = lax.all_gather(value_vectors, 'gx', axis=0, tiled=True)  25 us
    dot_general x4, matrix products, row_products(): jnp.dot(source, piece, preferred_element_type=jnp.float32)  21.2 us
    dot_general x1, matrix products, per_device(): jnp.dot(hidden, down_full, preferred_element_type=jnp.float32)  16.3 us
  transfers between devices with their start and end apart: 13, of which 10 were waited for; matrix products, arithmetic and copies ran while one was open for 10% of the time, Pallas kernels for 0%

profile of v1, /device:TPU:0, one launch (start us, length us, event | category | flops | bytes accessed | tf_op | source)
XLA Modules:
  0.0 525.0 jit_solution(14903019865644642604)
XLA Ops:
  9.1 1.8 fusion.23
  13.4 14.6 %all_gather.32 = bf16[4096,64]{0,1:T(8,128)(2,1)S(1)} all-gather(bf16[512,64]{0,1:T(8,128)(2,1)} %param.18), channel_id=1, replica_groups=mesh['gx'=8,'gy'=16] {'gx'}, dimensions={0}, use_global_device_ids=true | all-gather | bytes 589824 | tf_op jit(solution)/shard_map/all_gather | solution.py:95
  28.0 36.9 %all-gather.9.cloned.1.call-done = bf16[512,4096]{1,0:T(8,128)(2,1)} async-done(((bf16[32,4096]{1,0:T(8,128)(2,1)}), bf16[512,4096]{1,0:T(8,128)(2,1)}) %all-gather.9.cloned.1.call-update) | async-done | bytes 4194320 | tf_op jit(solution)/shard_map/all_gather | solution.py:87
  64.9 3.6 fusion.62
  68.5 1.5 collective-permute-start
  70.0 2.8 collective-permute-done
  74.2 14.2 %all_gather.34 = bf16[4096,64]{0,1:T(8,128)(2,1)S(1)} all-gather(bf16[512,64]{0,1:T(8,128)(2,1)S(1)} %copy-done.4), channel_id=1, replica_groups=mesh['gx'=8,'gy'=16] {'gx'}, dimensions={0}, use_global_device_ids=true | all-gather | bytes 589824 | tf_op jit(solution)/shard_map/all_gather | solution.py:96
  88.4 3.6 fusion.64
  92.0 1.8 collective-permute-start.1
  93.8 2.6 collective-permute-done.1
  97.9 3.6 fusion.20
  102.1 1.8 multiply_cosine_fusion
  103.9 4.2 fusion.63
  108.5 1.2 fusion.29
  109.9 7.8 %all-gather.13.cloned.1.call-done = bf16[4096,128]{0,1:T(8,128)(2,1)} async-done(((bf16[512,128]{0,1:T(8,128)(2,1)}), bf16[4096,128]{0,1:T(8,128)(2,1)}) %all-gather.13.cloned.1.call-update) | async-done | bytes 1048592 | tf_op jit(solution)/shard_map/all_gather | solution.py:124
  117.7 25.0 %all-gather.15.cloned.1.call-done = bf16[4096,128]{0,1:T(8,128)(2,1)} async-done(((bf16[512,128]{0,1:T(8,128)(2,1)}), bf16[4096,128]{0,1:T(8,128)(2,1)}) %all-gather.15.cloned.1.call-update) | async-done | bytes 1048592 | tf_op jit(solution)/shard_map/all_gather | solution.py:125
  142.8 14.2 %conditional.1 = (f32[1,2,512]{2,1,0:T(2,128)S(1)}, f32[1,2,512,128]{2,3,1,0:T(8,128)S(1)}) conditional(s32[]{:T(128)} %convert_element_type.114, () %tuple.16, (pred[512,4096]{0,1:T(8,128)(4,1)S(1)}, bf16[512,1,2,128]{3,0,2,1:T(8,128)(2,1)S(1)}, bf16[4096,128]{0,1:T(8,128)(2,1)}, bf16[4096,128]{0,1:T(8,128)(2,1)}) %tuple.17), branch_computations={%region_6.7_spmd, %region_7.10_spmd} | conditional | flops 2202008576 | bytes 63725612 | solution.py:154
  142.8 5.1 fusion
  147.9 4.6 fusion.7
  152.5 4.4 fusion.2
  157.0 12.6 %all-gather.17.cloned.1.call-done = bf16[256,4096]{1,0:T(8,128)(2,1)} async-done(((bf16[256,512]{1,0:T(8,128)(2,1)}), bf16[256,4096]{1,0:T(8,128)(2,1)}) %all-gather.17.cloned.1.call-update) | async-done | bytes 2097168 | tf_op jit(solution)/shard_map/all_gather | solution.py:159
  169.6 4.9 convolution_convert_fusion.1
  174.6 77.9 %reduce-scatter.3.cloned.1.call-done = bf16[32,4096]{1,0:T(8,128)(2,1)} async-done(((bf16[512,4096]{1,0:T(8,128)(2,1)}), bf16[32,4096]{1,0:T(8,128)(2,1)}) %reduce-scatter.3.cloned.1.call-update) | async-done | bytes 262160 | tf_op jit(solution)/shard_map/reduce_scatter | solution.py:162
  253.7 1.8 fusion.27
  258.0 112.9 %all_to_all.10 = bf16[8,512,896]{2,1,0:T(8,128)(2,1)} all-to-all(bf16[8,512,896]{2,1,0:T(8,128)(2,1)S(1)} %stack.8), channel_id=1, replica_groups=mesh['gx'=8,'gy'=16] {'gx'}, dimensions={0} | all-to-all | bytes 14680064 | tf_op jit(solution)/shard_map/all_to_all | solution.py:173
  370.9 9.9 %fusion.65 = f32[512,896]{1,0:T(8,128)S(1)} fusion(bf16[512,4096]{1,0:T(8,128)(2,1)} %all-gather.19.cloned.1.call-done, bf16[4096,896]{1,0:T(8,128)(2,1)} %bitcast.88), kind=kOutput, calls=%fused_computation.120 | convolution fusion | flops 3758096384 | bytes 13369344 | tf_op jit(solution)/shard_map/dot_general | solution.py:58
  380.8 41.6 %all-gather.23.cloned.1.call-done = bf16[896,4096]{1,0:T(8,128)(2,1)} async-done(((bf16[896,512]{1,0:T(8,128)(2,1)}), bf16[896,4096]{1,0:T(8,128)(2,1)}) %all-gather.23.cloned.1.call-update) | async-done | bytes 7340048 | tf_op jit(solution)/shard_map/all_gather | solution.py:179
  422.4 16.3 %convolution_convert_fusion = bf16[512,4096]{1,0:T(8,128)(2,1)} fusion(bf16[896,4096]{1,0:T(8,128)(2,1)} %all-gather.23.cloned.1.call-done, f32[512,896]{1,0:T(8,128)S(1)} %fusion.65, bf16[512,4096]{1,0:T(8,128)(2,1)} %all-gather.19.cloned.1.call-done, bf16[4096,896]{1,0:T(8,128)(2,1)} %all-gather.21.cloned.1.call-done), kind=kOutput, calls=%fused_computation.22 | convolution fusion | flops 7521042432 | bytes 24903680 | tf_op jit(solution)/shard_map/dot_general | solution.py:181
  441.8 3.4 all-to-all-start.1
  445.2 6.0 %all-to-all-done.1 = bf16[8,2,4096]{2,1,0:T(2,128)(2,1)S(1)} async-done(((bf16[8,2,4096]{2,1,0:T(2,128)(2,1)}), bf16[8,2,4096]{2,1,0:T(2,128)(2,1)S(1)}, u32[]{:S(2)}, u32[]{:S(2)}) %all-to-all-start.1) | async-done | bytes 131104 | tf_op jit(solution)/shard_map/all_to_all | solution.py:220
  453.1 63.3 %reduce-scatter.5.cloned.1.call-done = bf16[32,4096]{1,0:T(8,128)(2,1)} async-done(((bf16[512,4096]{1,0:T(8,128)(2,1)}), bf16[32,4096]{1,0:T(8,128)(2,1)}) %reduce-scatter.5.cloned.1.call-update) | async-done | bytes 262160 | tf_op jit(solution)/shard_map/reduce_scatter | solution.py:180
  516.4 1.7 fusion.28
  (89 shorter events, 16.3 us)
Async XLA Ops:
  7.2 57.7 %all-gather.9.cloned.1.call-start = ((), (), s32[]{:S(2)}) async-start(), calls=%async_computation.4 | async-start | bytes 4456448 | tf_op jit(solution)/shard_map/all_gather | solution.py:87
  7.9 66.3 %copy-start.4 = (bf16[512,64]{0,1:T(8,128)(2,1)S(1)}, bf16[512,64]{0,1:T(8,128)(2,1)}, u32[]{:S(2)}) copy-start(bf16[512,64]{0,1:T(8,128)(2,1)} %param.19) | copy-start | bytes 196612
  10.9 93.0 %all-gather.11.cloned.1.call-start = ((), (), s32[]{:S(2)}) async-start(), calls=%async_computation.5 | async-start | bytes 2359296 | tf_op jit(solution)/shard_map/all_gather | solution.py:90
  11.6 106.1 %all-gather.13.cloned.1.call-start = ((), (), s32[]{:S(2)}) async-start(), calls=%async_computation.6 | async-start | bytes 1179648 | tf_op jit(solution)/shard_map/all_gather | solution.py:124
  68.5 4.3 collective-permute-start
  74.1 68.7 %all-gather.15.cloned.1.call-start = ((), (), s32[]{:S(2)}) async-start(), calls=%async_computation.7 | async-start | bytes 1179648 | tf_op jit(solution)/shard_map/all_gather | solution.py:125
  92.0 4.4 collective-permute-start.1
  97.1 72.5 %all-gather.17.cloned.1.call-start = ((), (), s32[]{:S(2)}) async-start(), calls=%async_computation.8 | async-start | bytes 2359296 | tf_op jit(solution)/shard_map/all_gather | solution.py:159
  97.7 154.8 %reduce-scatter.3.cloned.1.call-start = ((), (), s32[]{:S(2)}) async-start(), calls=%async_computation.9 | async-start | bytes 4456448 | tf_op jit(solution)/shard_map/reduce_scatter | solution.py:162
  142.8 5.1 copy-start.7
  169.6 5.0 copy-start.5
  169.6 82.9 %copy-start = (bf16[32,4096]{1,0:T(8,128)(2,1)S(1)}, bf16[32,4096]{1,0:T(8,128)(2,1)}, u32[]{:S(2)}) copy-start(bf16[32,4096]{1,0:T(8,128)(2,1)} %param.14) | copy-start | bytes 786436
  174.5 82.5 %copy-start.2 = (bf16[512,896]{1,0:T(8,128)(2,1)S(1)}, bf16[512,896]{1,0:T(8,128)(2,1)}, u32[]{:S(2)}) copy-start(bf16[512,896]{1,0:T(8,128)(2,1)} %param.21) | copy-start | bytes 2752516
  174.5 196.4 %all-gather.19.cloned.1.call-start = ((), (), s32[]{:S(2)}) async-start(), calls=%async_computation.10 | async-start | bytes 4456448 | tf_op jit(solution)/shard_map/all_gather | solution.py:166
  255.5 125.3 %all-gather.21.cloned.1.call-start = ((), (), s32[]{:S(2)}) async-start(), calls=%async_computation.11 | async-start | bytes 8257536 | tf_op jit(solution)/shard_map/all_gather | solution.py:175
  256.2 166.2 %all-gather.23.cloned.1.call-start = ((), (), s32[]{:S(2)}) async-start(), calls=%async_computation.12 | async-start | bytes 8257536 | tf_op jit(solution)/shard_map/all_gather | solution.py:179
  257.0 259.4 %reduce-scatter.5.cloned.1.call-start = ((), (), s32[]{:S(2)}) async-start(), calls=%async_computation.13 | async-start | bytes 4456448 | tf_op jit(solution)/shard_map/reduce_scatter | solution.py:180
  438.7 0.7 copy-start.6
  438.7 1.2 copy-start.3
  438.7 77.7 %copy-start.1 = (bf16[32,4096]{1,0:T(8,128)(2,1)S(1)}, bf16[32,4096]{1,0:T(8,128)(2,1)}, u32[]{:S(2)}) copy-start(bf16[32,4096]{1,0:T(8,128)(2,1)} %reduce-scatter.3.cloned.1.call-done) | copy-start | bytes 786436
  441.8 9.4 %all-to-all-start.1 = ((bf16[8,2,4096]{2,1,0:T(2,128)(2,1)}), bf16[8,2,4096]{2,1,0:T(2,128)(2,1)S(1)}, u32[]{:S(2)}, u32[]{:S(2)}) async-start(bf16[8,2,4096]{2,1,0:T(2,128)(2,1)} %reshape.459), calls=%async_computation.3 | async-start | bytes 262144 | tf_op jit(solution)/shard_map/all_to_all | solution.py:220
Sparse Core Ops, SparseCore 0:
  11.0 53.8 all-gather.8
  66.6 25.7 all-gather.10
  94.1 23.5 all-gather.12
  119.3 23.4 all-gather.14
  144.3 25.2 all-gather.16
  174.7 77.8 reduce-scatter.2
  255.6 50.8 all-gather.18
  308.3 68.2 all-gather.20
  378.4 43.9 all-gather.22
  438.9 77.5 reduce-scatter.4
